TPU v7x, 256 devices: a whole 4x4x8 slice. The times are simulated.
256 devices in a mesh: grp: 8 (over y, x_hi), tok: 32 (over z, x_lo, core).
Axes of the slice: x: 4 (x_hi: 2, x_lo: 2; x = x_hi * 2 + x_lo), y: 4, z: 8, core: 2. Of those that a mesh axis runs over, the one named last changes fastest.
Arguments:
- layer_input: bfloat16 [8, 6144, 1536], P('grp', 'tok'), may hold values from -54 to 54
- attn_gain: float32 [1536], replicated, may hold values from 0.1 to 1.9
- w_query: bfloat16 [1536, 1536], P('tok'), may hold values from -0.15625 to 0.15625
- w_keyval: bfloat16 [1536, 1024], P('tok'), may hold values from -0.15625 to 0.15625
- w_output: bfloat16 [1536, 1536], P('tok'), may hold values from -0.15625 to 0.15625
- prefix_cache: bfloat16 [8, 512, 1024], P('grp', 'tok'), may hold values from -260 to 260
- lengths: int32 [8, 48], P('grp'), may hold values from 1 to 192, 6144 in all within a row
- moe_gain: float32 [1536], replicated, may hold values from 0.1 to 1.9
- w_router: bfloat16 [1536, 16], replicated, may hold values from -0.15625 to 0.15625
- routes: int32 [8, 6144, 2], P('grp', 'tok'), may hold values from 0 to 15, all different within a row; in each aligned block of 192 rows (0 to 191, 192 to 383, ..., all dimensions but the last counted through in order) at most 30 rows name the same one
- w_expert_in: bfloat16 [32, 1536, 1024], P('tok', 'grp'), may hold values from -0.15625 to 0.15625
- w_expert_out: bfloat16 [32, 512, 1536], P('tok', 'grp'), may hold values from -0.1875 to 0.1875
Outputs:
- hidden: bfloat16 [8, 6144, 1536], P('grp', 'tok')
- suffix_cache: bfloat16 [8, 6144, 1024], P('grp', 'tok')
Inputs may be any that keep to these rules, and one draw needn't show every extreme that they name: `lengths`: each row sums to 6144, and its largest length is 192. A token's 2 routes differ. Among the rows of one device no expert is named more than 30 times, a bound that some block reaches in some devices' rows.
All inputs are finite; a program needn't handle non-finite values.
Results may differ from a plain program's by a relative error of at most 0.0073.
The roundings to bfloat16 on the way count: a program that leaves them out, or rounds other values in their place, can miss the bound.
Values may be sent and summed in bfloat16 or wider, within the bound.
A program may use at most 64 MiB of HBM per device.

v0:
```python
import jax
import jax.numpy as jnp
from jax import lax
from jax.sharding import PartitionSpec as P

HEADS = 24
KV_HEADS = 8
HEAD_DIM = 64
TOP = 2
EPS = 1e-05


def passed_along(value, axis, steps):
    count = lax.axis_size(axis)
    initial, last = (max(0, -steps), min(count, count - steps))
    return lax.ppermute(value, axis, [(source, source + steps) for source in range(initial, last)])


def rms_scale(inputs, scale_row):
    inputs = inputs.astype(jnp.float32)
    inverse = lax.rsqrt(jnp.mean(inputs * inputs, axis=-1, keepdims=True) + EPS)
    return inputs * inverse * scale_row


def segment_of(req_lengths, positions):
    request_ends = jnp.cumsum(req_lengths, dtype=jnp.int32)
    return jnp.sum((request_ends[None, :] <= positions[:, None]).astype(jnp.int32), axis=1)


def product(left, right):
    return jnp.dot(left, right, preferred_element_type=jnp.float32)


def attend(soft_state, queries, key_block, allowed):
    maxima, totals, numerators = soft_state
    kv_width = key_block.shape[1] // 2
    key_rows = key_block[:, :kv_width].reshape(
        key_block.shape[0], queries.shape[1], queries.shape[3]
    )
    value_rows = key_block[:, kv_width:].reshape(
        key_block.shape[0], queries.shape[1], queries.shape[3]
    )
    scores = jnp.einsum(
        "tkgd,skd->tkgs", queries, key_rows, preferred_element_type=jnp.float32
    ) * queries.shape[3] ** (-0.5)
    if allowed is not None:
        scores = jnp.where(allowed[:, None, None, :], scores, -jnp.inf)
    new_max = jnp.maximum(maxima, jnp.max(scores, axis=-1))
    rescale = jnp.exp(maxima - new_max)
    weights = jnp.exp(scores - new_max[..., None])
    totals = totals * rescale + jnp.sum(weights, axis=-1)
    numerators = numerators * rescale[..., None] + jnp.einsum(
        "tkgs,skd->tkgd",
        weights.astype(jnp.bfloat16),
        value_rows,
        preferred_element_type=jnp.float32,
    )
    return (new_max, totals, numerators)


def on_device(
    layer_input,
    attn_gain,
    w_query,
    w_keyval,
    w_output,
    prefix_cache,
    lengths,
    moe_gain,
    w_router,
    routes,
    w_expert_in,
    w_expert_out,
):
    tokens = layer_input[0]
    row_count = tokens.shape[0]
    model_width = tokens.shape[1]
    group_share = HEADS // KV_HEADS
    normed = rms_scale(tokens, attn_gain).astype(jnp.bfloat16)
    columns = normed
    query_full = product(columns, lax.all_gather(w_query, "tok", axis=0, tiled=True))
    keyval_full = product(columns, lax.all_gather(w_keyval, "tok", axis=0, tiled=True))
    queries = query_full.astype(jnp.bfloat16).reshape(row_count, KV_HEADS, group_share, HEAD_DIM)
    keyval = keyval_full.astype(jnp.bfloat16)
    position = lax.axis_index("tok")
    positions = position * row_count + jnp.arange(row_count, dtype=jnp.int32)
    req_lengths = lengths[0]
    own_seg = segment_of(req_lengths, positions)
    before_seg = jnp.where(
        positions >= row_count, segment_of(req_lengths, positions - row_count), -1
    )
    earlier = passed_along(keyval, "tok", 1)
    near_block = jnp.concatenate([earlier, keyval], axis=0)
    near_seg = jnp.concatenate([before_seg, own_seg])
    near_pos = jnp.concatenate([positions - row_count, positions])
    allowed = (near_seg[None, :] == own_seg[:, None]) & (near_pos[None, :] <= positions[:, None])
    soft_state = (
        jnp.full((row_count, KV_HEADS, group_share), -jnp.inf, jnp.float32),
        jnp.zeros((row_count, KV_HEADS, group_share), jnp.float32),
        jnp.zeros((row_count, KV_HEADS, group_share, HEAD_DIM), jnp.float32),
    )
    soft_state = attend(soft_state, queries, near_block, allowed)
    prefix_whole = lax.all_gather(prefix_cache[0], "tok", axis=0, tiled=True)
    maxima, totals, numerators = attend(soft_state, queries, prefix_whole, None)
    attended = (
        (numerators / totals[..., None]).astype(jnp.bfloat16).reshape(row_count, HEADS * HEAD_DIM)
    )
    columns = attended
    residual = tokens.astype(jnp.float32) + product(
        columns, lax.all_gather(w_output, "tok", axis=0, tiled=True)
    )
    normed2 = rms_scale(residual, moe_gain).astype(jnp.bfloat16)
    logits = product(normed2, w_router)
    experts = w_router.shape[1]
    chosen = routes[0]
    expert_marks = chosen[:, :, None] == jnp.arange(experts, dtype=jnp.int32)
    picked = jnp.sum(jnp.where(expert_marks, logits[:, None, :], 0.0), axis=-1)
    scores = jax.nn.sigmoid(picked)
    gate_weights = scores / jnp.sum(scores, axis=-1, keepdims=True)
    capacity = max(4, 5 * row_count * TOP // (4 * experts))
    flat_routes = chosen.reshape(-1)
    flat_marks = expert_marks.reshape(-1, experts).astype(jnp.int32)
    prior_count = jnp.cumsum(flat_marks, axis=0, dtype=jnp.int32) - flat_marks
    slot_index = jnp.sum(prior_count * flat_marks, axis=1)
    target = flat_routes * capacity + slot_index
    copies = flat_routes.shape[0]
    slot_match = target[None, :] == jnp.arange(experts * capacity, dtype=jnp.int32)[:, None]
    filled = jnp.any(slot_match, axis=1)
    source = jnp.sum(jnp.where(slot_match, jnp.arange(copies, dtype=jnp.int32)[None, :], 0), axis=1)
    outgoing = jnp.where(filled[:, None], normed2[source // TOP], 0).reshape(
        experts, capacity, model_width
    )
    to_send = jnp.repeat(outgoing, 2, axis=0)
    arrived = lax.all_to_all(to_send, "tok", split_axis=0, concat_axis=0, tiled=True)
    flat_rows = arrived.reshape(-1, model_width)
    columns = flat_rows
    gate_up = product(columns, lax.all_gather(w_expert_in[0], "grp", axis=0, tiled=True))
    half_units = gate_up.shape[1] // 2
    act = (jax.nn.silu(gate_up[:, :half_units]) * gate_up[:, half_units:]).astype(jnp.bfloat16)
    columns = act
    partial_out = product(columns, lax.all_gather(w_expert_out[0], "grp", axis=0, tiled=True))
    returned = lax.all_to_all(
        partial_out.reshape(arrived.shape).astype(jnp.bfloat16),
        "tok",
        split_axis=0,
        concat_axis=0,
        tiled=True,
    ).astype(jnp.float32)
    results = jnp.sum(returned.reshape(experts, 2, capacity, model_width), axis=1).astype(
        jnp.bfloat16
    )
    gathered = results.reshape(experts * capacity, model_width)[target].astype(jnp.float32)
    weighted = jnp.sum(
        gathered.reshape(row_count, TOP, model_width) * gate_weights[:, :, None], axis=1
    )
    hidden = (residual + weighted).astype(jnp.bfloat16)
    return (hidden[None], keyval[None])


def solution(mesh):
    in_specs = (
        P("grp", "tok", None),
        P(),
        P("tok", None),
        P("tok", None),
        P("tok", None),
        P("grp", "tok", None),
        P("grp", None),
        P(),
        P(),
        P("grp", "tok", None),
        P("tok", "grp", None),
        P("tok", "grp", None),
    )
    out_specs = (P("grp", "tok", None), P("grp", "tok", None))
    return jax.shard_map(
        on_device, mesh=mesh, in_specs=in_specs, out_specs=out_specs, check_vma=False
    )
```

profile of v0, /device:TPU:1, one launch (start us, length us, event | category | flops | bytes accessed | tf_op | source)
XLA Modules:
  0.0 535.8 jit_solution(8123321330734562649)
XLA Ops:
  7.2 0.7 all-gather.10.cloned.1.call-update
  8.0 0.7 all-gather.16.cloned.1.call-update
  8.7 0.7 all-gather.12.cloned.1.call-update
  9.4 0.5 all-gather.14.cloned.1.call-update
  10.0 0.5 all-gather.18.cloned.1.call-update
  10.6 0.8 copy.41
  11.7 1.3 fusion.22
  13.0 0.7 copy.35
  14.0 0.9 reduce-window.19
  15.7 63.8 %all-gather.10.cloned.1.call-done = bf16[1536,1024]{1,0:T(8,128)(2,1)} async-done(((bf16[48,1024]{1,0:T(8,128)(2,1)}), bf16[1536,1024]{1,0:T(8,128)(2,1)}) %all-gather.10.cloned.1.call-update) | async-done | bytes 3145744 | tf_op jit(solution)/shard_map/all_gather | solution.py:82
  79.5 2.9 convolution_convert_fusion.2
  82.4 2.7 collective-permute-start
  85.4 59.2 %all-gather.16.cloned.1.call-done = bf16[1,512,1024]{2,1,0:T(8,128)(2,1)} async-done(((bf16[1,16,1024]{2,1,0:T(8,128)(2,1)}), bf16[1,512,1024]{2,1,0:T(8,128)(2,1)}) %all-gather.16.cloned.1.call-update) | async-done | bytes 1048592 | tf_op jit(solution)/shard_map/all_gather | solution.py:103
  144.6 1.3 fusion.42
  146.7 0.9 copy.38
  147.6 65.7 %all-gather.12.cloned.1.call-done = bf16[1536,1536]{1,0:T(8,128)(2,1)} async-done(((bf16[48,1536]{1,0:T(8,128)(2,1)}), bf16[1536,1536]{1,0:T(8,128)(2,1)}) %all-gather.12.cloned.1.call-update) | async-done | bytes 4718608 | tf_op jit(solution)/shard_map/all_gather | solution.py:81
  213.3 3.5 convolution_convert_fusion.1
  216.8 0.3 copy.37
  217.1 1.6 bitcast_reduce_fusion
  218.7 1.7 fusion.5
  220.3 2.4 fusion.1
  222.7 3.2 fusion.6
  226.0 2.3 fusion.3
  228.3 2.5 fusion.18
  230.8 51.3 %all-gather.14.cloned.1.call-done = bf16[1536,1536]{1,0:T(8,128)(2,1)} async-done(((bf16[48,1536]{1,0:T(8,128)(2,1)}), bf16[1536,1536]{1,0:T(8,128)(2,1)}) %all-gather.14.cloned.1.call-update) | async-done | bytes 4718608 | tf_op jit(solution)/shard_map/all_gather | solution.py:110
  282.1 3.6 multiply_reduce_fusion.1
  285.7 1.1 copy-done.1
  286.9 2.9 gather_fusion
  289.9 1.5 gather.9
  291.6 2.1 broadcast_in_dim.108
  293.7 6.4 %all-to-all-start = ((bf16[32,30,1536]{2,1,0:T(8,128)(2,1)}), bf16[32,30,1536]{2,1,0:T(8,128)(2,1)}, u32[]{:S(2)}, u32[]{:S(2)}) async-start(bf16[32,30,1536]{2,1,0:T(8,128)(2,1)} %bitcast.112), calls=%async_computation | async-start | bytes 6291456 | tf_op jit(solution)/shard_map/all_to_all | solution.py:134
  300.1 0.2 all-gather.20.cloned.1.call-start
  300.3 0.3 all-gather.20.cloned.1.call-update
  300.7 71.3 %all-to-all-done = bf16[32,30,1536]{2,1,0:T(8,128)(2,1)} async-done(((bf16[32,30,1536]{2,1,0:T(8,128)(2,1)}), bf16[32,30,1536]{2,1,0:T(8,128)(2,1)}, u32[]{:S(2)}, u32[]{:S(2)}) %all-to-all-start) | async-done | bytes 2949152 | tf_op jit(solution)/shard_map/all_to_all | solution.py:134
  372.0 4.4 reshape.322
  376.4 7.9 %fusion.13 = f32[960,1024]{1,0:T(8,128)} fusion(bf16[960,1536]{1,0:T(8,128)(2,1)} %reshape.322, bf16[1,1536,1024]{2,1,0:T(8,128)(2,1)} %all-gather.18.cloned.1.call-done), kind=kOutput, calls=%fused_computation.19 | convolution fusion | flops 3019898880 | bytes 10027008 | tf_op jit(solution)/shard_map/dot_general | solution.py:31
  384.3 40.2 %all-gather.20.cloned.1.call-done = bf16[1,512,1536]{2,1,0:T(8,128)(2,1)} async-done(((bf16[1,64,1536]{2,1,0:T(8,128)(2,1)}), bf16[1,512,1536]{2,1,0:T(8,128)(2,1)}) %all-gather.20.cloned.1.call-update) | async-done | bytes 1572880 | tf_op jit(solution)/shard_map/all_gather | solution.py:141
  424.5 5.9 %convolution_convert_fusion = bf16[960,1536]{1,0:T(8,128)(2,1)} fusion(bf16[1,512,1536]{2,1,0:T(8,128)(2,1)} %all-gather.20.cloned.1.call-done, f32[960,1024]{1,0:T(8,128)} %fusion.13), kind=kOutput, calls=%fused_computation.15 | convolution fusion | flops 1514373120 | bytes 8454144 | tf_op jit(solution)/shard_map/dot_general | solution.py:31
  430.5 4.5 convert_element_type.85
  434.9 9.0 %all-to-all-start.1 = ((bf16[32,30,1536]{2,1,0:T(8,128)(2,1)}), bf16[32,30,1536]{2,1,0:T(8,128)(2,1)}, u32[]{:S(2)}, u32[]{:S(2)}) async-start(bf16[32,30,1536]{2,1,0:T(8,128)(2,1)} %convert_element_type.85), calls=%async_computation.1 | async-start | bytes 6291456 | tf_op jit(solution)/shard_map/all_to_all | solution.py:142
  444.2 0.2 fusion.43
  444.7 71.1 %all-to-all-done.1 = bf16[32,30,1536]{2,1,0:T(8,128)(2,1)} async-done(((bf16[32,30,1536]{2,1,0:T(8,128)(2,1)}), bf16[32,30,1536]{2,1,0:T(8,128)(2,1)}, u32[]{:S(2)}, u32[]{:S(2)}) %all-to-all-start.1) | async-done | bytes 2949152 | tf_op jit(solution)/shard_map/all_to_all | solution.py:142
  515.8 2.5 bitcast_reduce_fusion.1
  518.3 0.4 convert_element_type.87
  518.7 2.8 gather_fusion.1
  521.5 2.8 reshape.326
  524.4 3.6 multiply_reduce_fusion
  528.0 0.9 fusion.28
  (63 shorter events, 3.4 us)
Async XLA Ops:
  7.2 437.1 %copy-start = (bf16[1536,16]{0,1:T(8,128)(2,1)S(1)}, bf16[1536,16]{0,1:T(8,128)(2,1)}, u32[]{:S(2)}) copy-start(bf16[1536,16]{0,1:T(8,128)(2,1)} %param.20) | copy-start | bytes 147460
  7.2 72.3 %all-gather.10.cloned.1.call-start = ((), (), s32[]{:S(2)}) async-start(), calls=%async_computation.2 | async-start | bytes 3244032 | tf_op jit(solution)/shard_map/all_gather | solution.py:82
  7.9 136.7 %all-gather.16.cloned.1.call-start = ((), (), s32[]{:S(2)}) async-start(), calls=%async_computation.5 | async-start | bytes 1081344 | tf_op jit(solution)/shard_map/all_gather | solution.py:103
  8.7 204.6 %all-gather.12.cloned.1.call-start = ((), (), s32[]{:S(2)}) async-start(), calls=%async_computation.3 | async-start | bytes 4866048 | tf_op jit(solution)/shard_map/all_gather | solution.py:81
  9.4 272.7 %all-gather.14.cloned.1.call-start = ((), (), s32[]{:S(2)}) async-start(), calls=%async_computation.4 | async-start | bytes 4866048 | tf_op jit(solution)/shard_map/all_gather | solution.py:110
  10.0 366.5 %all-gather.18.cloned.1.call-start = ((), (), s32[]{:S(2)}) async-start(), calls=%async_computation.6 | async-start | bytes 3538944 | tf_op jit(solution)/shard_map/all_gather | solution.py:137
  82.4 64.1 %copy-start.5 = (bf16[192,1024]{1,0:T(8,128)(2,1)}, bf16[192,1024]{1,0:T(8,128)(2,1)S(1)}, u32[]{:S(2)}) copy-start(bf16[192,1024]{1,0:T(8,128)(2,1)S(1)} %convolution_convert_fusion.2) | copy-start | bytes 1179652
  82.4 64.0 %collective-permute-start = (bf16[192,1024]{1,0:T(8,128)(2,1)S(1)}, bf16[192,1024]{1,0:T(8,128)(2,1)S(1)}, u32[]{:S(2)}, u32[]{:S(2)}) collective-permute-start(bf16[192,1024]{1,0:T(8,128)(2,1)S(1)} %convolution_convert_fusion.2), channel_id=1, source_target_pairs={{0,1},{1,2},{2,3},{3,4},{4,5},{5,6},{6,7},{7,8},{8,9},{9,10},{10,1... | collective-permute-start | bytes 1179656 | tf_op jit(solution)/shard_map/ppermute | solution.py:16
  145.9 67.4 %copy-start.3 = (bf16[1,192,1536]{2,1,0:T(8,128)(2,1)S(1)}, bf16[1,192,1536]{2,1,0:T(8,128)(2,1)}, u32[]{:S(2)}) copy-start(bf16[1,192,1536]{2,1,0:T(8,128)(2,1)} %param.12) | copy-start | bytes 1769476
  145.9 67.4 %copy-start.8 = (f32[1536]{0:T(1024)S(1)}, f32[1536]{0:T(1024)}, u32[]{:S(2)}) copy-start(f32[1536]{0:T(1024)} %param.13) | copy-start | bytes 18436
  226.0 2.3 copy-start.4
  282.1 4.7 copy-start.7
  285.7 1.1 copy-start.1
  293.7 78.3 %all-to-all-start = ((bf16[32,30,1536]{2,1,0:T(8,128)(2,1)}), bf16[32,30,1536]{2,1,0:T(8,128)(2,1)}, u32[]{:S(2)}, u32[]{:S(2)}) async-start(bf16[32,30,1536]{2,1,0:T(8,128)(2,1)} %bitcast.112), calls=%async_computation | async-start | bytes 6291456 | tf_op jit(solution)/shard_map/all_to_all | solution.py:134
  300.1 124.4 %all-gather.20.cloned.1.call-start = ((), (), s32[]{:S(2)}) async-start(), calls=%async_computation.7 | async-start | bytes 1769472 | tf_op jit(solution)/shard_map/all_gather | solution.py:141
  434.9 9.0 %copy-start.6 = (s32[1,192,2]{1,2,0:T(2,128)S(1)}, s32[1,192,2]{1,2,0:T(2,128)}, u32[]{:S(2)}) copy-start(s32[1,192,2]{1,2,0:T(2,128)} %param.21) | copy-start | bytes 4612
  434.9 80.9 %all-to-all-start.1 = ((bf16[32,30,1536]{2,1,0:T(8,128)(2,1)}), bf16[32,30,1536]{2,1,0:T(8,128)(2,1)}, u32[]{:S(2)}, u32[]{:S(2)}) async-start(bf16[32,30,1536]{2,1,0:T(8,128)(2,1)} %convert_element_type.85), calls=%async_computation.1 | async-start | bytes 6291456 | tf_op jit(solution)/shard_map/all_to_all | solution.py:142
  524.4 3.6 copy-start.2
Sparse Core Ops, SparseCore 0:
  9.8 69.5 all-gather.9
  81.3 63.2 all-gather.15
  146.5 66.7 all-gather.11
  215.0 67.0 all-gather.13
  284.5 88.3 all-gather.17
  375.4 49.0 all-gather.19
where the time goes:
time: 536 us
  waiting for transfers between devices  426 us (79%)
  matrix products  33 us (6%)
  local copies, waits for them, and re-layouts  28.2 us (5%)
  starting transfers between devices  18.5 us (3%)
  other arithmetic  15.3 us (3%)
  between operations  14.5 us (3%)
    all_to_all x1, waiting for transfers between devices, on_device(): lax.all_to_all(to_send, 'tok', split_axis=0, concat_axis=0, tiled=True)  71.3 us
    all_to_all x1, waiting for transfers between devices, on_device(): lax.all_to_all(partial_out.reshape(arrived.shape).astype(jnp.bfloat16), '...  71.1 us
    all_gather x1, waiting for transfers between devices, on_device(): lax.all_gather(w_query, 'tok', axis=0, tiled=True)  65.7 us
    all_gather x1, waiting for transfers between devices, on_device(): lax.all_gather(w_keyval, 'tok', axis=0, tiled=True)  63.8 us
    all_gather x1, waiting for transfers between devices, on_device(): prefix_whole = lax.all_gather(prefix_cache[0], 'tok', axis=0, tiled=True)  59.2 us
    all_gather x1, waiting for transfers between devices, on_device(): lax.all_gather(w_output, 'tok', axis=0, tiled=True)  51.3 us
    all_gather x1, waiting for transfers between devices, on_device(): lax.all_gather(w_expert_out[0], 'grp', axis=0, tiled=True)  40.2 us
    dot_general x6, matrix products, product(): return jnp.dot(left, right, preferred_element_type=jnp.float32)  24 us
  transfers between devices with their start and end apart: 9, of which 7 were waited for; matrix products, arithmetic and copies ran while one was open for 10% of the time, Pallas kernels for 0%

commit v1 on v0

--- a/solution.py
+++ b/solution.py
@@ -138,7 +138,12 @@
     half_units = gate_up.shape[1] // 2
     act = (jax.nn.silu(gate_up[:, :half_units]) * gate_up[:, half_units:]).astype(jnp.bfloat16)
     columns = act
-    partial_out = product(columns, lax.all_gather(w_expert_out[0], "grp", axis=0, tiled=True))
+    partial_out = product(
+        columns,
+        jnp.concatenate(
+            lax.all_to_all(jnp.stack([w_expert_out[0]] * lax.axis_size("grp")), "grp", 0, 0), axis=0
+        ),
+    )
     returned = lax.all_to_all(
         partial_out.reshape(arrived.shape).astype(jnp.bfloat16),
         "tok",

time: 536 us -> 515 us (0.961)
  waiting for transfers between devices: 426 us -> 396 us
  starting transfers between devices: 18.5 us -> 28.4 us
    all_gather x1 -> x0, waiting for transfers between devices: 40.2 us -> none  [on_device(): lax.all_gather(w_expert_out[0], 'grp', axis=0, tiled=True)]
    all_to_all x0 -> x1, waiting for transfers between devices: none -> 9.03 us  [on_device(): lax.all_to_all(jnp.stack([w_expert_out[0]] * lax.axis_size('grp')), 'grp'...]
    all_to_all x0 -> x1, starting transfers between devices: none -> 6.15 us  [on_device(): lax.all_to_all(jnp.stack([w_expert_out[0]] * lax.axis_size('grp')), 'grp'...]
  transfers between devices with their start and end apart: 9 -> 9, of which waited for: 7 -> 8; matrix products, arithmetic and copies ran while one was open for 10% -> 8% of each run, Pallas kernels for 0% -> 0%
where the time goes in v1:
time: 515 us; the launch traced here: 514 us
  waiting for transfers between devices  396 us (77%)
  local copies, waits for them, and re-layouts  29.6 us (6%)
  starting transfers between devices  28.4 us (6%)
  matrix products  28.2 us (5%)
  other arithmetic  16 us (3%)
  between operations  15.6 us (3%)
    all_to_all x1, waiting for transfers between devices, on_device(): lax.all_to_all(to_send, 'tok', split_axis=0, concat_axis=0, tiled=True)  71.3 us
    all_to_all x1, waiting for transfers between devices, on_device(): lax.all_to_all(partial_out.reshape(arrived.shape).astype(jnp.bfloat16), '...  71 us
    all_gather x1, waiting for transfers between devices, on_device(): lax.all_gather(w_query, 'tok', axis=0, tiled=True)  65.7 us
    all_gather x1, waiting for transfers between devices, on_device(): lax.all_gather(w_keyval, 'tok', axis=0, tiled=True)  64.4 us
    all_gather x1, waiting for transfers between devices, on_device(): prefix_whole = lax.all_gather(prefix_cache[0], 'tok', axis=0, tiled=True)  59.2 us
    all_gather x1, waiting for transfers between devices, on_device(): lax.all_gather(w_output, 'tok', axis=0, tiled=True)  51.1 us
    dot_general x6, matrix products, product(): return jnp.dot(left, right, preferred_element_type=jnp.float32)  19.2 us
    all_to_all x1, starting transfers between devices, on_device(): lax.all_to_all(partial_out.reshape(arrived.shape).astype(jnp.bfloat16), '...  12.7 us
  transfers between devices with their start and end apart: 9, of which 8 were waited for; matrix products, arithmetic and copies ran while one was open for 8% of the time, Pallas kernels for 0%

profile of v1, /device:TPU:1, one launch (start us, length us, event | category | flops | bytes accessed | tf_op | source)
XLA Modules:
  0.0 513.6 jit_solution(6288355232546390912)
XLA Ops:
  8.1 0.7 all-gather.8.cloned.1.call-update
  8.8 0.7 all-gather.14.cloned.1.call-update
  9.5 0.7 all-gather.10.cloned.1.call-update
  10.3 0.5 all-gather.12.cloned.1.call-update
  10.8 0.8 copy.59
  11.9 0.7 copy.53
  12.8 0.9 reduce-window.19
  14.4 1.3 fusion.21
  15.9 64.4 %all-gather.8.cloned.1.call-done = bf16[1536,1024]{1,0:T(8,128)(2,1)} async-done(((bf16[48,1024]{1,0:T(8,128)(2,1)}), bf16[1536,1024]{1,0:T(8,128)(2,1)}) %all-gather.8.cloned.1.call-update) | async-done | bytes 3145744 | tf_op jit(solution)/shard_map/all_gather | solution.py:82
  80.3 2.9 convolution_convert_fusion.2
  83.2 2.7 collective-permute-start
  86.3 59.2 %all-gather.14.cloned.1.call-done = bf16[1,512,1024]{2,1,0:T(8,128)(2,1)} async-done(((bf16[1,16,1024]{2,1,0:T(8,128)(2,1)}), bf16[1,512,1024]{2,1,0:T(8,128)(2,1)}) %all-gather.14.cloned.1.call-update) | async-done | bytes 1048592 | tf_op jit(solution)/shard_map/all_gather | solution.py:103
  145.5 1.3 fusion.39
  147.5 0.9 copy.56
  148.4 65.7 %all-gather.10.cloned.1.call-done = bf16[1536,1536]{1,0:T(8,128)(2,1)} async-done(((bf16[48,1536]{1,0:T(8,128)(2,1)}), bf16[1536,1536]{1,0:T(8,128)(2,1)}) %all-gather.10.cloned.1.call-update) | async-done | bytes 4718608 | tf_op jit(solution)/shard_map/all_gather | solution.py:81
  214.1 3.5 convolution_convert_fusion.1
  217.9 1.6 fusion.5
  219.5 1.6 bitcast_reduce_fusion
  221.2 2.3 fusion.3
  223.5 2.4 fusion.1
  225.9 3.2 fusion.6
  229.1 2.5 fusion.17
  231.7 51.1 %all-gather.12.cloned.1.call-done = bf16[1536,1536]{1,0:T(8,128)(2,1)} async-done(((bf16[48,1536]{1,0:T(8,128)(2,1)}), bf16[1536,1536]{1,0:T(8,128)(2,1)}) %all-gather.12.cloned.1.call-update) | async-done | bytes 4718608 | tf_op jit(solution)/shard_map/all_gather | solution.py:110
  282.8 3.6 multiply_reduce_fusion.1
  286.4 1.0 copy-done.1
  287.6 2.9 gather_fusion
  290.5 1.5 gather.9
  292.2 2.1 broadcast_in_dim.108
  294.3 6.6 %all-to-all-start = ((bf16[32,30,1536]{2,1,0:T(8,128)(2,1)}), bf16[32,30,1536]{2,1,0:T(8,128)(2,1)}, u32[]{:S(2)}, u32[]{:S(2)}) async-start(bf16[32,30,1536]{2,1,0:T(8,128)(2,1)} %bitcast.114), calls=%async_computation | async-start | bytes 6291456 | tf_op jit(solution)/shard_map/all_to_all | solution.py:134
  301.0 0.5 all-gather.16.cloned.1.call-update
  301.5 71.3 %all-to-all-done = bf16[32,30,1536]{2,1,0:T(8,128)(2,1)} async-done(((bf16[32,30,1536]{2,1,0:T(8,128)(2,1)}), bf16[32,30,1536]{2,1,0:T(8,128)(2,1)}, u32[]{:S(2)}, u32[]{:S(2)}) %all-to-all-start) | async-done | bytes 2949152 | tf_op jit(solution)/shard_map/all_to_all | solution.py:134
  372.8 1.3 stack.3
  374.1 6.1 %all-to-all-start.1 = ((bf16[8,64,1536]{2,1,0:T(8,128)(2,1)}), bf16[8,64,1536]{2,1,0:T(8,128)(2,1)S(1)}, u32[]{:S(2)}, u32[]{:S(2)}) async-start(bf16[8,64,1536]{2,1,0:T(8,128)(2,1)} %stack.3), calls=%async_computation.1 | async-start | bytes 3145728 | tf_op jit(solution)/shard_map/all_to_all | solution.py:144
  380.2 4.5 reshape.326
  384.8 0.7 all-gather.16.cloned.1.call-done
  385.5 6.0 %fusion.13 = f32[960,1024]{1,0:T(8,128)S(1)} fusion(bf16[960,1536]{1,0:T(8,128)(2,1)} %reshape.326, bf16[1,1536,1024]{2,1,0:T(8,128)(2,1)} %all-gather.16.cloned.1.call-done), kind=kOutput, calls=%fused_computation.19 | convolution fusion | flops 3019898880 | bytes 10027008 | tf_op jit(solution)/shard_map/dot_general | solution.py:31
  391.5 0.7 fusion.15
  392.1 1.3 dot_general.40
  393.4 9.0 %all-to-all-done.1 = bf16[8,64,1536]{2,1,0:T(8,128)(2,1)S(1)} async-done(((bf16[8,64,1536]{2,1,0:T(8,128)(2,1)}), bf16[8,64,1536]{2,1,0:T(8,128)(2,1)S(1)}, u32[]{:S(2)}, u32[]{:S(2)}) %all-to-all-start.1) | async-done | bytes 1572896 | tf_op jit(solution)/shard_map/all_to_all | solution.py:144
  402.4 3.1 convolution_convert_fusion
  405.5 3.3 copy.63
  408.8 12.7 %all-to-all-start.2 = ((bf16[32,30,1536]{2,1,0:T(8,128)(2,1)}), bf16[32,30,1536]{2,1,0:T(8,128)(2,1)}, u32[]{:S(2)}, u32[]{:S(2)}) async-start(bf16[32,30,1536]{2,1,0:T(8,128)(2,1)} %copy.63), calls=%async_computation.2 | async-start | bytes 6291456 | tf_op jit(solution)/shard_map/all_to_all | solution.py:147
  422.4 71.0 %all-to-all-done.2 = bf16[32,30,1536]{2,1,0:T(8,128)(2,1)} async-done(((bf16[32,30,1536]{2,1,0:T(8,128)(2,1)}), bf16[32,30,1536]{2,1,0:T(8,128)(2,1)}, u32[]{:S(2)}, u32[]{:S(2)}) %all-to-all-start.2) | async-done | bytes 2949152 | tf_op jit(solution)/shard_map/all_to_all | solution.py:147
  493.4 2.5 bitcast_reduce_fusion.1
  496.3 2.8 gather_fusion.1
  499.1 2.8 reshape.331
  502.0 3.6 multiply_reduce_fusion
  505.5 0.9 fusion.26
  (67 shorter events, 4.4 us)
Async XLA Ops:
  8.0 413.9 %copy-start = (bf16[1536,16]{0,1:T(8,128)(2,1)S(1)}, bf16[1536,16]{0,1:T(8,128)(2,1)}, u32[]{:S(2)}) copy-start(bf16[1536,16]{0,1:T(8,128)(2,1)} %param.20) | copy-start | bytes 147460
  8.0 72.3 %all-gather.8.cloned.1.call-start = ((), (), s32[]{:S(2)}) async-start(), calls=%async_computation.3 | async-start | bytes 3244032 | tf_op jit(solution)/shard_map/all_gather | solution.py:82
  8.7 136.7 %all-gather.14.cloned.1.call-start = ((), (), s32[]{:S(2)}) async-start(), calls=%async_computation.6 | async-start | bytes 1081344 | tf_op jit(solution)/shard_map/all_gather | solution.py:103
  9.5 204.6 %all-gather.10.cloned.1.call-start = ((), (), s32[]{:S(2)}) async-start(), calls=%async_computation.4 | async-start | bytes 4866048 | tf_op jit(solution)/shard_map/all_gather | solution.py:81
  10.2 272.6 %all-gather.12.cloned.1.call-start = ((), (), s32[]{:S(2)}) async-start(), calls=%async_computation.5 | async-start | bytes 4866048 | tf_op jit(solution)/shard_map/all_gather | solution.py:110
  83.2 64.0 %copy-start.5 = (bf16[192,1024]{1,0:T(8,128)(2,1)}, bf16[192,1024]{1,0:T(8,128)(2,1)S(1)}, u32[]{:S(2)}) copy-start(bf16[192,1024]{1,0:T(8,128)(2,1)S(1)} %convolution_convert_fusion.2) | copy-start | bytes 1179652
  83.2 64.0 %collective-permute-start = (bf16[192,1024]{1,0:T(8,128)(2,1)S(1)}, bf16[192,1024]{1,0:T(8,128)(2,1)S(1)}, u32[]{:S(2)}, u32[]{:S(2)}) collective-permute-start(bf16[192,1024]{1,0:T(8,128)(2,1)S(1)} %convolution_convert_fusion.2), channel_id=1, source_target_pairs={{0,1},{1,2},{2,3},{3,4},{4,5},{5,6},{6,7},{7,8},{8,9},{9,10},{10,1... | collective-permute-start | bytes 1179656 | tf_op jit(solution)/shard_map/ppermute | solution.py:16
  147.0 67.2 %copy-start.3 = (bf16[1,192,1536]{2,1,0:T(8,128)(2,1)S(1)}, bf16[1,192,1536]{2,1,0:T(8,128)(2,1)}, u32[]{:S(2)}) copy-start(bf16[1,192,1536]{2,1,0:T(8,128)(2,1)} %param.12) | copy-start | bytes 1769476
  147.0 67.2 %copy-start.9 = (f32[1536]{0:T(1024)S(1)}, f32[1536]{0:T(1024)}, u32[]{:S(2)}) copy-start(f32[1536]{0:T(1024)} %param.13) | copy-start | bytes 18436
  225.9 3.2 copy-start.4
  282.8 4.6 copy-start.8
  286.4 1.0 copy-start.1
  294.3 78.5 %copy-start.6 = (bf16[1,64,1536]{2,1,0:T(8,128)(2,1)S(1)}, bf16[1,64,1536]{2,1,0:T(8,128)(2,1)}, u32[]{:S(2)}) copy-start(bf16[1,64,1536]{2,1,0:T(8,128)(2,1)} %param.23) | copy-start | bytes 589828
  294.3 78.5 %all-to-all-start = ((bf16[32,30,1536]{2,1,0:T(8,128)(2,1)}), bf16[32,30,1536]{2,1,0:T(8,128)(2,1)}, u32[]{:S(2)}, u32[]{:S(2)}) async-start(bf16[32,30,1536]{2,1,0:T(8,128)(2,1)} %bitcast.114), calls=%async_computation | async-start | bytes 6291456 | tf_op jit(solution)/shard_map/all_to_all | solution.py:134
  300.9 84.6 %all-gather.16.cloned.1.call-start = ((), (), s32[]{:S(2)}) async-start(), calls=%async_computation.7 | async-start | bytes 3538944 | tf_op jit(solution)/shard_map/all_gather | solution.py:137
  374.1 28.3 %all-to-all-start.1 = ((bf16[8,64,1536]{2,1,0:T(8,128)(2,1)}), bf16[8,64,1536]{2,1,0:T(8,128)(2,1)S(1)}, u32[]{:S(2)}, u32[]{:S(2)}) async-start(bf16[8,64,1536]{2,1,0:T(8,128)(2,1)} %stack.3), calls=%async_computation.1 | async-start | bytes 3145728 | tf_op jit(solution)/shard_map/all_to_all | solution.py:144
  408.8 12.7 %copy-start.7 = (s32[1,192,2]{1,2,0:T(2,128)S(1)}, s32[1,192,2]{1,2,0:T(2,128)}, u32[]{:S(2)}) copy-start(s32[1,192,2]{1,2,0:T(2,128)} %param.21) | copy-start | bytes 4612
  408.8 84.6 %all-to-all-start.2 = ((bf16[32,30,1536]{2,1,0:T(8,128)(2,1)}), bf16[32,30,1536]{2,1,0:T(8,128)(2,1)}, u32[]{:S(2)}, u32[]{:S(2)}) async-start(bf16[32,30,1536]{2,1,0:T(8,128)(2,1)} %copy.63), calls=%async_computation.2 | async-start | bytes 6291456 | tf_op jit(solution)/shard_map/all_to_all | solution.py:147
  502.0 3.6 copy-start.2
Sparse Core Ops, SparseCore 0:
  10.7 69.5 all-gather.7
  82.2 63.2 all-gather.13
  147.3 66.7 all-gather.9
  215.8 66.9 all-gather.11
Sparse Core Ops, SparseCore 1:
  304.0 81.5 all-gather.15
